TPU v7x, 128 devices: a whole 4x4x4 slice. The times are simulated.
128 devices in a mesh: grp: 2 (over y_hi), row: 8 (over z, y_lo), col: 8 (over x, core).
Axes of the slice: x: 4, y: 4 (y_hi: 2, y_lo: 2; y = y_hi * 2 + y_lo), z: 4, core: 2. Of those that a mesh axis runs over, the one named last changes fastest.
Arguments:
- queries: bfloat16 [8192, 2048], P(('row', 'col'), 'grp'), parts along dimension 1, may hold values from -102 to 102
- keys: bfloat16 [8192, 256], P(('col', 'row'), 'grp'), parts along dimension 1, may hold values from -5 to 5
- values: bfloat16 [8192, 256], P(('col', 'row'), 'grp'), parts along dimension 1, may hold values from -6 to 6
- span_order: int32 [64], replicated, may hold values from 0 to 63, each once
Outputs:
- attended: float32 [8192, 2048], P(('row', 'col'), 'grp'), parts along dimension 1
There are 2 independent parts, one for each index of `grp`. A program takes and returns all parts, laid end to end along the dimension named above; an argument that names none is the same for every part. Nothing has to cross between parts.
All inputs are finite; a program needn't handle non-finite values.
Results may differ from a plain program's by a relative error of at most 0.0022.
Values may be sent and summed in bfloat16 or wider, within the bound.
No kernel may reach another device: no remote copies, remote signals or barrier semaphores. Data moves between devices by JAX's collectives and lax.ppermute only.
A program may use at most 64 MiB of HBM per device.

v0:
```python
import functools
import math

import jax
import jax.numpy as jnp
from jax import lax
from jax.experimental import pallas as pl
from jax.experimental.pallas import tpu as pltpu
from jax.sharding import PartitionSpec as P

HEADS = 8
HD = 128
SPAN = 128
ROWS = HEADS * SPAN
GROUP = 4
BLOCK = GROUP * SPAN
NEVER = -1e30
FLOOR = -1e29
SCALE = math.log2(math.e) / math.sqrt(HD)
VMEM = pltpu.VMEM
AXES = ("row", "col")


def place(z, y, x, core):
    return (z % 4 * 2 + y % 2) * 8 + x % 4 * 2 + core


def coords(index):
    row, col = divmod(index, 8)
    return row // 2, row % 2, col // 2, col % 2


def moved(to):
    return [(i, place(*to(*coords(i)))) for i in range(64)]


def along_a(step):
    return moved(lambda z, y, x, c: (z + step, y, x, c) if c == 0 else (z, y, x + step, c))


def along_b(step):
    return moved(lambda z, y, x, c: (z, y, x + step, c) if c == 0 else (z + step, y, x, c))


ACROSS_Y = moved(lambda z, y, x, c: (z, 1 - y, x, c))
ACROSS_CORE = moved(lambda z, y, x, c: (z, y, x, 1 - c))


def send(x, perm):
    return lax.ppermute(x, AXES, perm)


def whole(space=VMEM):
    return pl.BlockSpec(memory_space=space)


def limit(mib):
    return pltpu.CompilerParams(vmem_limit_bytes=mib << 20)


def cost(flops, moved_bytes, exps=0):
    return pl.CostEstimate(flops=flops, bytes_accessed=moved_bytes, transcendentals=exps)


NEAR_A = (0, -1, 1, 2)
FAR_B = (-1, 1, 2)
SLOTS = tuple((a, b) for b in (0, *FAR_B) for a in NEAR_A)
OWN, PARTNER, BESIDE, BESIDE_PARTNER = range(4)
NEAR = len(NEAR_A)
LISTS = (
    (OWN, 0, len(SLOTS)),
    (PARTNER, 0, len(SLOTS)),
    (BESIDE, NEAR, len(SLOTS)),
    (BESIDE_PARTNER, NEAR, len(SLOTS)),
    (BESIDE, 0, NEAR),
    (BESIDE_PARTNER, 0, NEAR),
)
KINDS = 32
STEPS = 63


def lists_kernel(order_ref, table_ref):
    row, col = lax.axis_index("row"), lax.axis_index("col")
    z, y, x, core = row >> 1, row & 1, col >> 1, col & 1
    first = core == 0
    at_a, at_b = jnp.where(first, z, x), jnp.where(first, x, z)
    wide_a, wide_b = jnp.where(first, 2, 16), jnp.where(first, 16, 2)
    part_a = {a: ((at_a + a) & 3) * wide_a + core * 8 + y for a in NEAR_A}
    part_b = {b: ((at_b + b) & 3) * wide_b for b in (0, *FAR_B)}
    theirs = [order_ref[part_a[a] + part_b[b]] for a, b in SLOTS]
    for u, (which, begin, end) in enumerate(LISTS):
        to_y = y if which < BESIDE else 1 - y
        to_core = core if which % 2 == 0 else 1 - core
        mine = order_ref[(z * 2 + to_y) * 8 + x * 2 + to_core]
        used = jnp.int32(0)
        for slot, order in list(enumerate(theirs))[begin:end]:
            table_ref[u, used] = slot
            table_ref[u, KINDS + used] = jnp.where(order == mine, 0, -SPAN)
            used = used + (order <= mine).astype(jnp.int32)
        for extra in range(GROUP):
            table_ref[u, used + extra] = begin
            table_ref[u, KINDS + used + extra] = SPAN
        table_ref[u, STEPS] = (used + GROUP - 1) >> 2


def lists(span_order):
    return pl.pallas_call(
        lists_kernel,
        out_shape=jax.ShapeDtypeStruct((len(LISTS), STEPS + 1), jnp.int32),
        in_specs=[whole(pltpu.SMEM)],
        out_specs=whole(pltpu.SMEM),
        compiler_params=limit(1),
        name="lists",
        cost_estimate=cost(1024, 1024),
    )(span_order)


def split_queries(queries_ref, q_ref):
    for head in range(HEADS):
        q = queries_ref[:, head * HD : (head + 1) * HD].astype(jnp.float32) * SCALE
        high = q.astype(jnp.bfloat16)
        rows = slice(head * SPAN, (head + 1) * SPAN)
        q_ref[rows, :HD] = high
        q_ref[rows, HD:] = (q - high.astype(jnp.float32)).astype(jnp.bfloat16)


def above_diagonal():
    return lax.broadcasted_iota(jnp.int32, (SPAN, SPAN), 0) - lax.broadcasted_iota(jnp.int32, (SPAN, SPAN), 1)


def keys_of(table_ref, u, kv_ref, step, columns):
    spans = [table_ref[u, step * GROUP + g] for g in range(GROUP)]
    parts = [kv_ref[pl.ds(pl.multiple_of(s * SPAN, SPAN), SPAN), columns] for s in spans]
    return jnp.concatenate(parts, axis=0)


def score_step(table_ref, u, kv_ref, q_ref, step, above, s_ref, top_ref):
    k = keys_of(table_ref, u, kv_ref, step, slice(0, HD))
    s = lax.dot_general(
        q_ref[...], jnp.concatenate([k, k], axis=1), (((1,), (1,)), ((), ())), preferred_element_type=jnp.float32
    )
    tiles = []
    for g in range(GROUP):
        allowed = above >= table_ref[u, KINDS + step * GROUP + g]
        tile = s[:, g * SPAN : (g + 1) * SPAN].reshape(HEADS, SPAN, SPAN)
        tiles.append(jnp.where(allowed[None], tile, NEVER).reshape(ROWS, SPAN))
    s_ref[...] = jnp.concatenate(tiles, axis=1)
    top_ref[...] = functools.reduce(jnp.maximum, tiles)


def absorb_step(table_ref, u, kv_ref, step, s_ref, top_ref, m_ref, acc_ref):
    old = m_ref[...]
    new = jnp.maximum(old, jnp.max(top_ref[...], axis=1, keepdims=True))
    fade = jnp.exp2(old - new)
    m_ref[...] = new
    weights = jnp.exp2(s_ref[...] - jnp.concatenate([new] * GROUP, axis=1)).astype(jnp.bfloat16)
    v = keys_of(table_ref, u, kv_ref, step, slice(HD, 2 * HD))
    v = jnp.concatenate([v, jnp.ones((BLOCK, HD), jnp.bfloat16)], axis=1)
    more = jnp.dot(weights, v, preferred_element_type=jnp.float32)
    acc_ref[...] = acc_ref[...] * jnp.concatenate([fade, fade], axis=1) + more


def near_kernel(lists_of, table_ref, *refs):
    count = len(lists_of)
    query_refs, kv_ref, refs = refs[:count], refs[count], refs[count + 1 :]
    m_refs, acc_refs, (q_ref, s_ref, top_ref) = refs[:count], refs[count : 2 * count], refs[2 * count :]
    above = above_diagonal()
    for i in range(count):
        split_queries(query_refs[i], q_ref.at[i])
        m_refs[i][...] = jnp.full((ROWS, HD), FLOOR, jnp.float32)
        acc_refs[i][...] = jnp.zeros((ROWS, 2 * HD), jnp.float32)
    for i, u in enumerate(lists_of):
        score_step(table_ref, u, kv_ref, q_ref.at[i], 0, above, s_ref.at[i], top_ref.at[i])
    for i, u in enumerate(lists_of):
        absorb_step(table_ref, u, kv_ref, 0, s_ref.at[i], top_ref.at[i], m_refs[i], acc_refs[i])


def attend_near(lists_of, table, queries, kv):
    count = len(lists_of)
    states = [jax.ShapeDtypeStruct((ROWS, HD), jnp.float32)] * count
    states += [jax.ShapeDtypeStruct((ROWS, 2 * HD), jnp.float32)] * count
    out = pl.pallas_call(
        functools.partial(near_kernel, lists_of),
        out_shape=states,
        in_specs=[whole(pltpu.SMEM)] + [whole()] * (count + 1),
        out_specs=[whole()] * (2 * count),
        scratch_shapes=[
            VMEM((count, ROWS, 2 * HD), jnp.bfloat16),
            VMEM((count, ROWS, BLOCK), jnp.float32),
            VMEM((count, ROWS, HD), jnp.float32),
        ],
        compiler_params=limit(24),
        cost_estimate=cost(4 * count * NEAR * ROWS * SPAN * HD, count * NEAR * SPAN * SPAN * 4, count * ROWS * BLOCK),
    )(table, *queries, kv)
    return list(zip(out[:count], out[count:]))


def attend_kernel(u, arrays, begun, table_ref, queries_ref, *refs):
    kv_refs, refs = refs[:arrays], refs[arrays:]
    if begun:
        m_in, acc_in, *refs = refs
    out_ref, *refs = refs
    if arrays > 1:
        kv_ref, *refs = refs
        at = 0
        for ref in kv_refs:
            kv_ref[at : at + ref.shape[0], :] = ref[...]
            at += ref.shape[0]
    else:
        kv_ref = kv_refs[0]
    q_ref, s_ref, top_ref, m_ref, acc_ref = refs
    total = table_ref[u, STEPS]

    split_queries(queries_ref, q_ref)
    if begun:
        m_ref[...] = m_in[...]
        acc_ref[...] = acc_in[...]
    else:
        m_ref[...] = jnp.full((ROWS, HD), FLOOR, jnp.float32)
        acc_ref[...] = jnp.zeros((ROWS, 2 * HD), jnp.float32)
    above = above_diagonal()

    def score(step, half):
        score_step(table_ref, u, kv_ref, q_ref, step, above, s_ref.at[half], top_ref.at[half])

    def absorb(step, half):
        absorb_step(table_ref, u, kv_ref, step, s_ref.at[half], top_ref.at[half], m_ref, acc_ref)

    @pl.when(total > 0)
    def _():
        score(0, 0)

        def two(pair, carry):
            step = 2 * pair
            score(step + 1, 1)
            absorb(step, 0)
            score(step + 2, 0)
            absorb(step + 1, 1)
            return carry

        lax.fori_loop(0, (total - 1) >> 1, two, 0)

        @pl.when(total % 2 == 1)
        def _():
            absorb(total - 1, 0)

        @pl.when(total % 2 == 0)
        def _():
            score(total - 1, 1)
            absorb(total - 2, 0)
            absorb(total - 1, 1)

    low = lax.broadcasted_iota(jnp.int32, (ROWS, HD), 1) < HD // 2
    out_ref[:ROWS, :] = acc_ref[:, :HD]
    out_ref[ROWS:, :] = jnp.where(low, m_ref[...], acc_ref[:, HD:])


def attend(u, table, queries, arrays, state=()):
    count = len(SLOTS)
    out = [jax.ShapeDtypeStruct((2 * ROWS, HD), jnp.float32)]
    if len(arrays) > 1:
        out.append(jax.ShapeDtypeStruct((count * SPAN, 2 * HD), jnp.bfloat16))
    return pl.pallas_call(
        functools.partial(attend_kernel, u, len(arrays), len(state) > 0),
        out_shape=out,
        in_specs=[whole(pltpu.SMEM)] + [whole()] * (1 + len(arrays) + len(state)),
        out_specs=[whole()] * len(out),
        scratch_shapes=[
            VMEM((ROWS, 2 * HD), jnp.bfloat16),
            VMEM((2, ROWS, BLOCK), jnp.float32),
            VMEM((2, ROWS, HD), jnp.float32),
            VMEM((ROWS, HD), jnp.float32),
            VMEM((ROWS, 2 * HD), jnp.float32),
        ],
        compiler_params=limit(24),
        cost_estimate=cost(4 * count * ROWS * SPAN * HD, count * SPAN * SPAN * 4, count * ROWS * SPAN),
    )(table, queries, *arrays, *state)


def lower_lanes():
    return lax.broadcasted_iota(jnp.int32, (SPAN, HD), 1) < HD // 2


def spread(packed):
    turned = pltpu.roll(packed, HD // 2, 1)
    low = lower_lanes()
    return jnp.where(low, packed, turned), jnp.where(low, turned, packed)


def join_kernel(near_ref, far_ref, out_ref):
    lane = lax.broadcasted_iota(jnp.int32, (SPAN, HD), 1)
    logs = jnp.zeros((SPAN, HD), jnp.bfloat16)
    for head in range(HEADS):
        rows = slice(head * SPAN, (head + 1) * SPAN)
        also = slice(ROWS + head * SPAN, ROWS + (head + 1) * SPAN)
        near, near_total = spread(near_ref[also, :])
        far, far_total = spread(far_ref[also, :])
        top = jnp.maximum(near, far)
        near, far = jnp.exp2(near - top), jnp.exp2(far - top)
        value = near_ref[rows, :] * near + far_ref[rows, :] * far
        weight = near_total * near + far_total * far
        live = weight > 0
        safe = jnp.where(live, weight, 1.0)
        out_ref[:, head * HD : (head + 1) * HD] = jnp.where(live, value / safe, 0.0).astype(jnp.bfloat16)
        rest = jnp.where(live, top + jnp.log(safe) * math.log2(math.e), NEVER)
        for part in range(3):
            piece = rest.astype(jnp.bfloat16)
            logs = jnp.where(lane == part * HEADS + head, piece, logs)
            rest = rest - piece.astype(jnp.float32)
    out_ref[:, HEADS * HD :] = logs


def joined(near, far):
    return pl.pallas_call(
        join_kernel,
        out_shape=jax.ShapeDtypeStruct((SPAN, (HEADS + 1) * HD), jnp.bfloat16),
        in_specs=[whole()] * 2,
        out_specs=whole(),
        compiler_params=limit(8),
        name="join",
        cost_estimate=cost(8 * ROWS * HD, 20 * ROWS * HD, 2 * ROWS * HD),
    )(near, far)


def merge_kernel(near_ref, far_ref, beside_ref, out_ref):
    parts = beside_ref[:, HEADS * HD :].astype(jnp.float32)
    logs = parts + pltpu.roll(parts, HD - HEADS, 1) + pltpu.roll(parts, HD - 2 * HEADS, 1)
    for head in range(HEADS):
        rows = slice(head * SPAN, (head + 1) * SPAN)
        also = slice(ROWS + head * SPAN, ROWS + (head + 1) * SPAN)
        columns = slice(head * HD, (head + 1) * HD)
        near, near_total = spread(near_ref[also, :])
        far, far_total = spread(far_ref[also, :])
        beside = jnp.broadcast_to(logs[:, head : head + 1], (SPAN, HD))
        top = jnp.maximum(jnp.maximum(near, far), beside)
        near, far, beside = jnp.exp2(near - top), jnp.exp2(far - top), jnp.exp2(beside - top)
        value = near_ref[rows, :] * near + far_ref[rows, :] * far + beside_ref[:, columns].astype(jnp.float32) * beside
        out_ref[:, columns] = value / (near_total * near + far_total * far + beside)


def merged(near, far, beside):
    return pl.pallas_call(
        merge_kernel,
        out_shape=jax.ShapeDtypeStruct((SPAN, HEADS * HD), jnp.float32),
        in_specs=[whole()] * 3,
        out_specs=whole(),
        compiler_params=limit(8),
        name="merge",
        cost_estimate=cost(8 * ROWS * HD, 20 * ROWS * HD, 2 * ROWS * HD),
    )(near, far, beside)


def together(keys, values):
    first = lax.broadcasted_iota(jnp.int32, (SPAN, 2 * HD), 1) < HD
    return jnp.where(first, jnp.pad(keys, ((0, 0), (0, HD))), jnp.pad(values, ((0, 0), (HD, 0))))


def attention(queries, keys, values, span_order):
    beside = send(queries, ACROSS_Y)
    kv = together(keys, values)
    by_a, by_b = {}, {}
    for d in (2, -1, 1):
        by_a[d] = send(kv, along_a(-d))
    table = lists(span_order)
    beside_partner = send(beside, ACROSS_CORE)
    plane = jnp.concatenate([kv, *(by_a[d] for d in NEAR_A[1:])], axis=0)
    for d in (2, -1, 1):
        by_b[d] = send(plane, along_b(-d))
    first, second = attend_near((5, 4), table, (beside_partner, beside), plane)
    partner = send(queries, ACROSS_CORE)

    arrays = [plane, *(by_b[d] for d in FAR_B)]
    far, held = attend(BESIDE_PARTNER, table, beside_partner, arrays, first)
    far = send(far, ACROSS_CORE)
    (near,) = attend(BESIDE, table, beside, [held], second)
    back = send(joined(near, far), ACROSS_Y)
    (far,) = attend(PARTNER, table, partner, [held])
    far = send(far, ACROSS_CORE)
    (near,) = attend(OWN, table, queries, [held])
    return merged(near, far, back)


def solution(mesh):
    placed = (P(("row", "col"), "grp"), P(("col", "row"), "grp"), P(("col", "row"), "grp"), P())
    return jax.shard_map(attention, mesh=mesh, in_specs=placed, out_specs=P(("row", "col"), "grp"), check_vma=False)
```

profile of v0, /device:TPU:0, one launch (start us, length us, event | category | flops | bytes accessed | tf_op | source)
XLA Modules:
  0.0 45.3 jit_solution(14513746986516194524)
XLA Ops:
  0.0 1.7 %collective-permute-start = (bf16[128,1024]{1,0:T(8,128)(2,1)}, bf16[128,1024]{1,0:T(8,128)(2,1)S(1)}, u32[]{:S(2)}, u32[]{:S(2)}) collective-permute-start(bf16[128,1024]{1,0:T(8,128)(2,1)} %queries_ref.1), channel_id=1, source_target_pairs={{0,8},{1,9},{2,10},{3,11},{4,12},{5,13},{6,14},{7,15},{8,0},{9,1},... | collective-permute-start | bytes 786440 | tf_op jit(solution)/shard_map/ppermute | solution.py:50
  1.7 0.8 %pad_select_fusion = bf16[128,256]{1,0:T(8,128)(2,1)S(1)} fusion(bf16[128,128]{1,0:T(8,128)(2,1)} %param.6, bf16[128,128]{1,0:T(8,128)(2,1)} %param.5, pred[256]{0:T(512)(128)(4,1)S(1)} %iota_compare_fusion), kind=kLoop, calls=%fused_computation.1 | loop fusion | flops 32768 | bytes 131328 | tf_op jit(solution)/shard_map/jit(_where)/select_n | solution.py:355
  2.5 0.0 copy-start.1
  2.5 0.0 copy-start
  2.5 2.0 %collective-permute-start.2 = (bf16[128,256]{1,0:T(8,128)(2,1)S(1)}, bf16[128,256]{1,0:T(8,128)(2,1)S(1)}, u32[]{:S(2)}, u32[]{:S(2)}) collective-permute-start(bf16[128,256]{1,0:T(8,128)(2,1)S(1)} %pad_select_fusion), channel_id=1, source_target_pairs={{0,16},{1,3},{2,18},{3,5},{4,20},{5,7},{6,22},{7,1},{8,24},{9,11},... | collective-permute-start | bytes 196616 | tf_op jit(solution)/shard_map/ppermute | solution.py:50
  4.5 2.2 %collective-permute-start.3 = (bf16[128,256]{1,0:T(8,128)(2,1)S(1)}, bf16[128,256]{1,0:T(8,128)(2,1)S(1)}, u32[]{:S(2)}, u32[]{:S(2)}) collective-permute-start(bf16[128,256]{1,0:T(8,128)(2,1)S(1)} %pad_select_fusion), channel_id=1, source_target_pairs={{0,48},{1,7},{2,50},{3,1},{4,52},{5,3},{6,54},{7,5},{8,56},{9,15},... | collective-permute-start | bytes 196616 | tf_op jit(solution)/shard_map/ppermute | solution.py:50
  6.7 1.8 %collective-permute-start.4 = (bf16[128,256]{1,0:T(8,128)(2,1)S(1)}, bf16[128,256]{1,0:T(8,128)(2,1)S(1)}, u32[]{:S(2)}, u32[]{:S(2)}) collective-permute-start(bf16[128,256]{1,0:T(8,128)(2,1)S(1)} %pad_select_fusion), channel_id=1, source_target_pairs={{0,32},{1,5},{2,34},{3,7},{4,36},{5,1},{6,38},{7,3},{8,40},{9,13},... | collective-permute-start | bytes 196616 | tf_op jit(solution)/shard_map/ppermute | solution.py:50
  8.5 0.0 collective-permute-done.refs_1_.queries_ref
  8.5 0.0 collective-permute-start.1
  8.5 0.4 collective-permute-done.2
  8.9 0.0 collective-permute-done.3
  8.9 3.6 %collective-permute-done.4 = bf16[128,256]{1,0:T(8,128)(2,1)S(1)} collective-permute-done((bf16[128,256]{1,0:T(8,128)(2,1)S(1)}, bf16[128,256]{1,0:T(8,128)(2,1)S(1)}, u32[]{:S(2)}, u32[]{:S(2)}) %collective-permute-start.4) | collective-permute-done | bytes 65568 | tf_op jit(solution)/shard_map/ppermute | solution.py:50
  12.5 1.6 %collective-permute-start.5 = (bf16[512,256]{1,0:T(8,128)(2,1)S(1)}, bf16[512,256]{1,0:T(8,128)(2,1)S(1)}, u32[]{:S(2)}, u32[]{:S(2)}) collective-permute-start(bf16[512,256]{1,0:T(8,128)(2,1)S(1)} %pad_maximum_fusion.refs_2_.refs_0_), channel_id=1, source_target_pairs={{0,2},{1,17},{2,4},{3,19},{4,6},{5,21},{6,0},{7,23},{8,10},{9,25},... | collective-permute-start | bytes 786440 | tf_op jit(solution)/shard_map/ppermute | solution.py:50
  14.1 1.7 %collective-permute-start.6 = (bf16[512,256]{1,0:T(8,128)(2,1)S(1)}, bf16[512,256]{1,0:T(8,128)(2,1)S(1)}, u32[]{:S(2)}, u32[]{:S(2)}) collective-permute-start(bf16[512,256]{1,0:T(8,128)(2,1)S(1)} %pad_maximum_fusion.refs_2_.refs_0_), channel_id=1, source_target_pairs={{0,6},{1,49},{2,0},{3,51},{4,2},{5,53},{6,4},{7,55},{8,14},{9,57},... | collective-permute-start | bytes 786440 | tf_op jit(solution)/shard_map/ppermute | solution.py:50
  15.8 1.8 %collective-permute-start.7 = (bf16[512,256]{1,0:T(8,128)(2,1)S(1)}, bf16[512,256]{1,0:T(8,128)(2,1)S(1)}, u32[]{:S(2)}, u32[]{:S(2)}) collective-permute-start(bf16[512,256]{1,0:T(8,128)(2,1)S(1)} %pad_maximum_fusion.refs_2_.refs_0_), channel_id=1, source_target_pairs={{0,4},{1,33},{2,6},{3,35},{4,0},{5,37},{6,2},{7,39},{8,12},{9,41},... | collective-permute-start | bytes 786440 | tf_op jit(solution)/shard_map/ppermute | solution.py:50
  17.6 0.0 copy-done.1
  17.6 0.0 collective-permute-start.8
  17.6 0.0 copy-done
  17.6 1.7 %lists.1.table_ref = s32[6,64]{1,0:T(8,128)S(1)} custom-call(s32[64]{0:T(128)S(1)} %copy-done), custom_call_target="tpu_custom_call" | custom-call | flops 1024 | bytes 1024 | tf_op jit(solution)/shard_map/lists/pallas_call | solution.py:107
  19.3 0.0 collective-permute-done.1.refs_0_.queries_ref
  19.3 2.5 %shard_map.46 = (f32[1024,128]{1,0:T(8,128)S(1)}, f32[1024,128]{1,0:T(8,128)S(1)}, f32[1024,256]{1,0:T(8,128)S(1)}, f32[1024,256]{1,0:T(8,128)S(1)}) custom-call(s32[6,64]{1,0:T(8,128)S(1)} %lists.1.table_ref, bf16[128,1024]{1,0:T(8,128)(2,1)S(1)} %collective-permute-done.1.refs_0_.queries_ref, ...), custom_call_target="tpu_custom_call" | custom-call | flops 536870912 | bytes 524288 | tf_op jit(solution)/shard_map/pallas_call | solution.py:182
  21.8 0.0 collective-permute-done.5.refs_1_
  21.8 0.8 %collective-permute-done.6.refs_2_ = bf16[512,256]{1,0:T(8,128)(2,1)S(1)} collective-permute-done((bf16[512,256]{1,0:T(8,128)(2,1)S(1)}, bf16[512,256]{1,0:T(8,128)(2,1)S(1)}, u32[]{:S(2)}, u32[]{:S(2)}) %collective-permute-start.6) | collective-permute-done | bytes 262176 | tf_op jit(solution)/shard_map/ppermute | solution.py:50
  22.5 1.4 %collective-permute-done.7.refs_3_ = bf16[512,256]{1,0:T(8,128)(2,1)S(1)} collective-permute-done((bf16[512,256]{1,0:T(8,128)(2,1)S(1)}, bf16[512,256]{1,0:T(8,128)(2,1)S(1)}, u32[]{:S(2)}, u32[]{:S(2)}) %collective-permute-start.7) | collective-permute-done | bytes 262176 | tf_op jit(solution)/shard_map/ppermute | solution.py:50
  23.9 2.7 %shard_map.47 = (f32[2048,128]{1,0:T(8,128)S(1)}, bf16[2048,256]{1,0:T(8,128)(2,1)S(1)}) custom-call(s32[6,64]{1,0:T(8,128)S(1)} %lists.1.table_ref, bf16[128,1024]{1,0:T(8,128)(2,1)S(1)} %collective-permute-done.1.refs_0_.queries_ref, bf16[512,256]{1,0:T(8,128)(2,1)S(1)} %pad_maximum_fusion.refs_2_.refs_0_, ...), custom_call_target="tpu_custom_call" | custom-call | flops 1073741824 | bytes 1048576 | tf_op jit(solution)/shard_map/pallas_call | solution.py:263
  26.6 0.1 collective-permute-start.10
  26.7 0.0 collective-permute-done.8.queries_ref
  26.7 2.1 %shard_map.49 = f32[2048,128]{1,0:T(8,128)S(1)} custom-call(s32[6,64]{1,0:T(8,128)S(1)} %lists.1.table_ref, bf16[128,1024]{1,0:T(8,128)(2,1)S(1)} %collective-permute-done.8.queries_ref, bf16[2048,256]{1,0:T(8,128)(2,1)S(1)} %get-tuple-element.13.refs_0_), custom_call_target="tpu_custom_call" | custom-call | flops 1073741824 | bytes 1048576 | tf_op jit(solution)/shard_map/pallas_call | solution.py:263
  28.9 2.0 %collective-permute-start.9 = (f32[2048,128]{1,0:T(8,128)S(1)}, f32[2048,128]{1,0:T(8,128)S(1)}, u32[]{:S(2)}, u32[]{:S(2)}) collective-permute-start(f32[2048,128]{1,0:T(8,128)S(1)} %shard_map.49), channel_id=1, source_target_pairs={{0,1},{1,0},{2,3},{3,2},{4,5},{5,4},{6,7},{7,6},{8,9},{9,8},{10,11... | collective-permute-start | bytes 3145736 | tf_op jit(solution)/shard_map/ppermute | solution.py:50
  30.9 2.6 %shard_map.50.near_ref = f32[2048,128]{1,0:T(8,128)S(1)} custom-call(s32[6,64]{1,0:T(8,128)S(1)} %lists.1.table_ref, bf16[128,1024]{1,0:T(8,128)(2,1)S(1)} %collective-permute-done.refs_1_.queries_ref, bf16[2048,256]{1,0:T(8,128)(2,1)S(1)} %get-tuple-element.13.refs_0_, f32[1024,128]{1,0:T(8,128)S(1)} %get-tuple-element.14.refs_1_, ...), custom_call_target="tpu_custom_call" | custom-call | flops 1073741824 | bytes 1048576 | tf_op jit(solution)/shard_map/pallas_call | solution.py:263
  33.5 0.0 collective-permute-done.10.far_ref
  33.5 0.7 %join.1 = bf16[128,1152]{1,0:T(8,128)(2,1)S(1)} custom-call(f32[2048,128]{1,0:T(8,128)S(1)} %shard_map.50.near_ref, f32[2048,128]{1,0:T(8,128)S(1)} %collective-permute-done.10.far_ref), custom_call_target="tpu_custom_call" | custom-call | flops 1048576 | bytes 2621440 | tf_op jit(solution)/shard_map/join/pallas_call | solution.py:314
  34.2 0.1 collective-permute-start.11
  34.3 3.4 %shard_map.48.near_ref = f32[2048,128]{1,0:T(8,128)S(1)} custom-call(s32[6,64]{1,0:T(8,128)S(1)} %lists.1.table_ref, bf16[128,1024]{1,0:T(8,128)(2,1)S(1)} %copy-done.1, bf16[2048,256]{1,0:T(8,128)(2,1)S(1)} %get-tuple-element.13.refs_0_), custom_call_target="tpu_custom_call" | custom-call | flops 1073741824 | bytes 1048576 | tf_op jit(solution)/shard_map/pallas_call | solution.py:263
  37.7 0.0 collective-permute-done.9.far_ref
  37.7 6.2 %collective-permute-done.11.beside_ref = bf16[128,1152]{1,0:T(8,128)(2,1)S(1)} collective-permute-done((bf16[128,1152]{1,0:T(8,128)(2,1)S(1)}, bf16[128,1152]{1,0:T(8,128)(2,1)S(1)}, u32[]{:S(2)}, u32[]{:S(2)}) %collective-permute-start.11) | collective-permute-done | bytes 294944 | tf_op jit(solution)/shard_map/ppermute | solution.py:50
  43.9 1.4 %merge.1 = f32[128,1024]{1,0:T(8,128)} custom-call(f32[2048,128]{1,0:T(8,128)S(1)} %shard_map.48.near_ref, f32[2048,128]{1,0:T(8,128)S(1)} %collective-permute-done.9.far_ref, bf16[128,1152]{1,0:T(8,128)(2,1)S(1)} %collective-permute-done.11.beside_ref), custom_call_target="tpu_custom_call" | custom-call | flops 1048576 | bytes 2621440 | tf_op jit(solution)/shard_map/merge/pallas_call | solution.py:342
  (2 shorter events, 0.0 us)
Async XLA Ops:
  0.0 8.5 %collective-permute-start = (bf16[128,1024]{1,0:T(8,128)(2,1)}, bf16[128,1024]{1,0:T(8,128)(2,1)S(1)}, u32[]{:S(2)}, u32[]{:S(2)}) collective-permute-start(bf16[128,1024]{1,0:T(8,128)(2,1)} %queries_ref.1), channel_id=1, source_target_pairs={{0,8},{1,9},{2,10},{3,11},{4,12},{5,13},{6,14},{7,15},{8,0},{9,1},... | collective-permute-start | bytes 786440 | tf_op jit(solution)/shard_map/ppermute | solution.py:50
  2.5 15.1 %copy-start.1 = (bf16[128,1024]{1,0:T(8,128)(2,1)S(1)}, bf16[128,1024]{1,0:T(8,128)(2,1)}, u32[]{:S(2)}) copy-start(bf16[128,1024]{1,0:T(8,128)(2,1)} %queries_ref.1) | copy-start | bytes 786436
  2.5 15.1 %copy-start = (s32[64]{0:T(128)S(1)}, s32[64]{0:T(128)}, u32[]{:S(2)}) copy-start(s32[64]{0:T(128)} %order_ref.1) | copy-start | bytes 772
  2.5 6.4 %collective-permute-start.2 = (bf16[128,256]{1,0:T(8,128)(2,1)S(1)}, bf16[128,256]{1,0:T(8,128)(2,1)S(1)}, u32[]{:S(2)}, u32[]{:S(2)}) collective-permute-start(bf16[128,256]{1,0:T(8,128)(2,1)S(1)} %pad_select_fusion), channel_id=1, source_target_pairs={{0,16},{1,3},{2,18},{3,5},{4,20},{5,7},{6,22},{7,1},{8,24},{9,11},... | collective-permute-start | bytes 196616 | tf_op jit(solution)/shard_map/ppermute | solution.py:50
  4.5 4.4 %collective-permute-start.3 = (bf16[128,256]{1,0:T(8,128)(2,1)S(1)}, bf16[128,256]{1,0:T(8,128)(2,1)S(1)}, u32[]{:S(2)}, u32[]{:S(2)}) collective-permute-start(bf16[128,256]{1,0:T(8,128)(2,1)S(1)} %pad_select_fusion), channel_id=1, source_target_pairs={{0,48},{1,7},{2,50},{3,1},{4,52},{5,3},{6,54},{7,5},{8,56},{9,15},... | collective-permute-start | bytes 196616 | tf_op jit(solution)/shard_map/ppermute | solution.py:50
  6.7 5.8 %collective-permute-start.4 = (bf16[128,256]{1,0:T(8,128)(2,1)S(1)}, bf16[128,256]{1,0:T(8,128)(2,1)S(1)}, u32[]{:S(2)}, u32[]{:S(2)}) collective-permute-start(bf16[128,256]{1,0:T(8,128)(2,1)S(1)} %pad_select_fusion), channel_id=1, source_target_pairs={{0,32},{1,5},{2,34},{3,7},{4,36},{5,1},{6,38},{7,3},{8,40},{9,13},... | collective-permute-start | bytes 196616 | tf_op jit(solution)/shard_map/ppermute | solution.py:50
  8.5 10.8 %collective-permute-start.1 = (bf16[128,1024]{1,0:T(8,128)(2,1)S(1)}, bf16[128,1024]{1,0:T(8,128)(2,1)S(1)}, u32[]{:S(2)}, u32[]{:S(2)}) collective-permute-start(bf16[128,1024]{1,0:T(8,128)(2,1)S(1)} %collective-permute-done.refs_1_.queries_ref), channel_id=1, source_target_pairs={{0,1},{1,0},{2,3},{3,2},{4,5},{5,4},{6,7},{7,6},{8,9},{9,8},{10,11... | collective-permute-start | bytes 786440 | tf_op jit(solution)/shard_map/ppermute | solution.py:50
  12.5 9.3 %collective-permute-start.5 = (bf16[512,256]{1,0:T(8,128)(2,1)S(1)}, bf16[512,256]{1,0:T(8,128)(2,1)S(1)}, u32[]{:S(2)}, u32[]{:S(2)}) collective-permute-start(bf16[512,256]{1,0:T(8,128)(2,1)S(1)} %pad_maximum_fusion.refs_2_.refs_0_), channel_id=1, source_target_pairs={{0,2},{1,17},{2,4},{3,19},{4,6},{5,21},{6,0},{7,23},{8,10},{9,25},... | collective-permute-start | bytes 786440 | tf_op jit(solution)/shard_map/ppermute | solution.py:50
  14.1 8.5 %collective-permute-start.6 = (bf16[512,256]{1,0:T(8,128)(2,1)S(1)}, bf16[512,256]{1,0:T(8,128)(2,1)S(1)}, u32[]{:S(2)}, u32[]{:S(2)}) collective-permute-start(bf16[512,256]{1,0:T(8,128)(2,1)S(1)} %pad_maximum_fusion.refs_2_.refs_0_), channel_id=1, source_target_pairs={{0,6},{1,49},{2,0},{3,51},{4,2},{5,53},{6,4},{7,55},{8,14},{9,57},... | collective-permute-start | bytes 786440 | tf_op jit(solution)/shard_map/ppermute | solution.py:50
  15.8 8.1 %collective-permute-start.7 = (bf16[512,256]{1,0:T(8,128)(2,1)S(1)}, bf16[512,256]{1,0:T(8,128)(2,1)S(1)}, u32[]{:S(2)}, u32[]{:S(2)}) collective-permute-start(bf16[512,256]{1,0:T(8,128)(2,1)S(1)} %pad_maximum_fusion.refs_2_.refs_0_), channel_id=1, source_target_pairs={{0,4},{1,33},{2,6},{3,35},{4,0},{5,37},{6,2},{7,39},{8,12},{9,41},... | collective-permute-start | bytes 786440 | tf_op jit(solution)/shard_map/ppermute | solution.py:50
  17.6 9.1 %collective-permute-start.8 = (bf16[128,1024]{1,0:T(8,128)(2,1)S(1)}, bf16[128,1024]{1,0:T(8,128)(2,1)S(1)}, u32[]{:S(2)}, u32[]{:S(2)}) collective-permute-start(bf16[128,1024]{1,0:T(8,128)(2,1)S(1)} %copy-done.1), channel_id=1, source_target_pairs={{0,1},{1,0},{2,3},{3,2},{4,5},{5,4},{6,7},{7,6},{8,9},{9,8},{10,11... | collective-permute-start | bytes 786440 | tf_op jit(solution)/shard_map/ppermute | solution.py:50
  26.6 6.8 %collective-permute-start.10 = (f32[2048,128]{1,0:T(8,128)S(1)}, f32[2048,128]{1,0:T(8,128)S(1)}, u32[]{:S(2)}, u32[]{:S(2)}) collective-permute-start(f32[2048,128]{1,0:T(8,128)S(1)} %get-tuple-element.16), channel_id=1, source_target_pairs={{0,1},{1,0},{2,3},{3,2},{4,5},{5,4},{6,7},{7,6},{8,9},{9,8},{10,11... | collective-permute-start | bytes 3145736 | tf_op jit(solution)/shard_map/ppermute | solution.py:50
  28.9 8.8 %collective-permute-start.9 = (f32[2048,128]{1,0:T(8,128)S(1)}, f32[2048,128]{1,0:T(8,128)S(1)}, u32[]{:S(2)}, u32[]{:S(2)}) collective-permute-start(f32[2048,128]{1,0:T(8,128)S(1)} %shard_map.49), channel_id=1, source_target_pairs={{0,1},{1,0},{2,3},{3,2},{4,5},{5,4},{6,7},{7,6},{8,9},{9,8},{10,11... | collective-permute-start | bytes 3145736 | tf_op jit(solution)/shard_map/ppermute | solution.py:50
  34.2 9.7 %collective-permute-start.11 = (bf16[128,1152]{1,0:T(8,128)(2,1)S(1)}, bf16[128,1152]{1,0:T(8,128)(2,1)S(1)}, u32[]{:S(2)}, u32[]{:S(2)}) collective-permute-start(bf16[128,1152]{1,0:T(8,128)(2,1)S(1)} %join.1), channel_id=1, source_target_pairs={{0,8},{1,9},{2,10},{3,11},{4,12},{5,13},{6,14},{7,15},{8,0},{9,1},... | collective-permute-start | bytes 884744 | tf_op jit(solution)/shard_map/ppermute | solution.py:50
where the time goes:
time: 46.2 us; the launch traced here: 45.3 us
  Pallas kernels  17 us (37%)
  starting transfers between devices  14.9 us (32%)
  waiting for transfers between devices  12.4 us (27%)
  other arithmetic  0.81 us (2%)
    ppermute x12, starting transfers between devices, send(): return lax.ppermute(x, AXES, perm)  14.9 us
    ppermute x12, waiting for transfers between devices, send(): return lax.ppermute(x, AXES, perm)  12.4 us
    pallas_call x4, Pallas kernels, attend(): pl.pallas_call(functools.partial(attend_kernel, u, len(arrays), len(state...  10.8 us
    pallas_call x1, Pallas kernels, attend_near(): pl.pallas_call(functools.partial(near_kernel, lists_of), out_shape=states...  2.45 us
    pallas_call x1, Pallas kernels, lists(): pl.pallas_call(lists_kernel, out_shape=jax.ShapeDtypeStruct((len(LISTS),...  1.66 us
    pallas_call x1, Pallas kernels, merged(): pl.pallas_call(merge_kernel, out_shape=jax.ShapeDtypeStruct((SPAN, HEADS...  1.42 us
  transfers between devices with their start and end apart: 12, of which 5 were waited for; matrix products, arithmetic and copies ran while one was open for 2% of the time, Pallas kernels for 34%

commit v1 on v0

--- a/solution.py
+++ b/solution.py
@@ -70,10 +70,12 @@
 LISTS = (
     (OWN, 0, len(SLOTS)),
     (PARTNER, 0, len(SLOTS)),
-    (BESIDE, NEAR, len(SLOTS)),
-    (BESIDE_PARTNER, NEAR, len(SLOTS)),
+    (BESIDE, NEAR, 3 * NEAR),
+    (BESIDE_PARTNER, NEAR, 3 * NEAR),
     (BESIDE, 0, NEAR),
     (BESIDE_PARTNER, 0, NEAR),
+    (BESIDE, 3 * NEAR, len(SLOTS)),
+    (BESIDE_PARTNER, 3 * NEAR, len(SLOTS)),
 )
 KINDS = 32
 STEPS = 63
@@ -100,7 +102,7 @@
         for extra in range(GROUP):
             table_ref[u, used + extra] = begin
             table_ref[u, KINDS + used + extra] = SPAN
-        table_ref[u, STEPS] = (used + GROUP - 1) >> 2
+        table_ref[u, STEPS] = (used + 1) >> 1
 
 
 def lists(span_order):
@@ -128,74 +130,82 @@
     return lax.broadcasted_iota(jnp.int32, (SPAN, SPAN), 0) - lax.broadcasted_iota(jnp.int32, (SPAN, SPAN), 1)
 
 
-def keys_of(table_ref, u, kv_ref, step, columns):
-    spans = [table_ref[u, step * GROUP + g] for g in range(GROUP)]
+def keys_of(table_ref, u, kv_ref, step, columns, begin, size):
+    spans = [table_ref[u, step * GROUP + g] - begin for g in range(size)]
     parts = [kv_ref[pl.ds(pl.multiple_of(s * SPAN, SPAN), SPAN), columns] for s in spans]
     return jnp.concatenate(parts, axis=0)
 
 
-def score_step(table_ref, u, kv_ref, q_ref, step, above, s_ref, top_ref):
-    k = keys_of(table_ref, u, kv_ref, step, slice(0, HD))
+def score_step(table_ref, u, kv_ref, q_ref, step, above, s_ref, top_ref, begin=0, size=GROUP):
+    k = keys_of(table_ref, u, kv_ref, step, slice(0, HD), begin, size)
     s = lax.dot_general(
         q_ref[...], jnp.concatenate([k, k], axis=1), (((1,), (1,)), ((), ())), preferred_element_type=jnp.float32
     )
     tiles = []
-    for g in range(GROUP):
+    for g in range(size):
         allowed = above >= table_ref[u, KINDS + step * GROUP + g]
         tile = s[:, g * SPAN : (g + 1) * SPAN].reshape(HEADS, SPAN, SPAN)
         tiles.append(jnp.where(allowed[None], tile, NEVER).reshape(ROWS, SPAN))
-    s_ref[...] = jnp.concatenate(tiles, axis=1)
+    s_ref[:, : size * SPAN] = jnp.concatenate(tiles, axis=1)
     top_ref[...] = functools.reduce(jnp.maximum, tiles)
 
 
-def absorb_step(table_ref, u, kv_ref, step, s_ref, top_ref, m_ref, acc_ref):
+def absorb_step(table_ref, u, kv_ref, step, s_ref, top_ref, m_ref, acc_ref, begin=0, size=GROUP):
     old = m_ref[...]
     new = jnp.maximum(old, jnp.max(top_ref[...], axis=1, keepdims=True))
     fade = jnp.exp2(old - new)
     m_ref[...] = new
-    weights = jnp.exp2(s_ref[...] - jnp.concatenate([new] * GROUP, axis=1)).astype(jnp.bfloat16)
-    v = keys_of(table_ref, u, kv_ref, step, slice(HD, 2 * HD))
-    v = jnp.concatenate([v, jnp.ones((BLOCK, HD), jnp.bfloat16)], axis=1)
+    scores = s_ref[:, : size * SPAN]
+    weights = jnp.exp2(scores - jnp.concatenate([new] * size, axis=1)).astype(jnp.bfloat16)
+    v = keys_of(table_ref, u, kv_ref, step, slice(HD, 2 * HD), begin, size)
+    v = jnp.concatenate([v, jnp.ones((size * SPAN, HD), jnp.bfloat16)], axis=1)
     more = jnp.dot(weights, v, preferred_element_type=jnp.float32)
     acc_ref[...] = acc_ref[...] * jnp.concatenate([fade, fade], axis=1) + more
 
 
-def near_kernel(lists_of, table_ref, *refs):
+def early_kernel(lists_of, begin, begun, table_ref, *refs):
     count = len(lists_of)
     query_refs, kv_ref, refs = refs[:count], refs[count], refs[count + 1 :]
-    m_refs, acc_refs, (q_ref, s_ref, top_ref) = refs[:count], refs[count : 2 * count], refs[2 * count :]
+    if begun:
+        m_in, acc_in, refs = refs[:count], refs[count : 2 * count], refs[2 * count :]
+    m_refs, acc_refs, refs = refs[:count], refs[count : 2 * count], refs[2 * count :]
+    *q_refs, s_ref, top_ref = refs
+    q_refs = query_refs if begun else refs[:count]
     above = above_diagonal()
     for i in range(count):
-        split_queries(query_refs[i], q_ref.at[i])
-        m_refs[i][...] = jnp.full((ROWS, HD), FLOOR, jnp.float32)
-        acc_refs[i][...] = jnp.zeros((ROWS, 2 * HD), jnp.float32)
+        if begun:
+            m_refs[i][...] = m_in[i][...]
+            acc_refs[i][...] = acc_in[i][...]
+        else:
+            split_queries(query_refs[i], q_refs[i])
+            m_refs[i][...] = jnp.full((ROWS, HD), FLOOR, jnp.float32)
+            acc_refs[i][...] = jnp.zeros((ROWS, 2 * HD), jnp.float32)
     for i, u in enumerate(lists_of):
-        score_step(table_ref, u, kv_ref, q_ref.at[i], 0, above, s_ref.at[i], top_ref.at[i])
+        score_step(table_ref, u, kv_ref, q_refs[i], 0, above, s_ref.at[i], top_ref.at[i], begin)
     for i, u in enumerate(lists_of):
-        absorb_step(table_ref, u, kv_ref, 0, s_ref.at[i], top_ref.at[i], m_refs[i], acc_refs[i])
-
-
-def attend_near(lists_of, table, queries, kv):
+        absorb_step(table_ref, u, kv_ref, 0, s_ref.at[i], top_ref.at[i], m_refs[i], acc_refs[i], begin)
+
+
+def attend_early(lists_of, begin, table, queries, kv, states=()):
     count = len(lists_of)
-    states = [jax.ShapeDtypeStruct((ROWS, HD), jnp.float32)] * count
-    states += [jax.ShapeDtypeStruct((ROWS, 2 * HD), jnp.float32)] * count
+    held = [m for m, _ in states] + [acc for _, acc in states]
+    out = [jax.ShapeDtypeStruct((ROWS, HD), jnp.float32)] * count
+    out += [jax.ShapeDtypeStruct((ROWS, 2 * HD), jnp.float32)] * count
+    if not held:
+        out += [jax.ShapeDtypeStruct((ROWS, 2 * HD), jnp.bfloat16)] * count
     out = pl.pallas_call(
-        functools.partial(near_kernel, lists_of),
-        out_shape=states,
-        in_specs=[whole(pltpu.SMEM)] + [whole()] * (count + 1),
-        out_specs=[whole()] * (2 * count),
-        scratch_shapes=[
-            VMEM((count, ROWS, 2 * HD), jnp.bfloat16),
-            VMEM((count, ROWS, BLOCK), jnp.float32),
-            VMEM((count, ROWS, HD), jnp.float32),
-        ],
+        functools.partial(early_kernel, lists_of, begin, len(held) > 0),
+        out_shape=out,
+        in_specs=[whole(pltpu.SMEM)] + [whole()] * (count + 1 + len(held)),
+        out_specs=[whole()] * len(out),
+        scratch_shapes=[VMEM((count, ROWS, BLOCK), jnp.float32), VMEM((count, ROWS, HD), jnp.float32)],
         compiler_params=limit(24),
         cost_estimate=cost(4 * count * NEAR * ROWS * SPAN * HD, count * NEAR * SPAN * SPAN * 4, count * ROWS * BLOCK),
-    )(table, *queries, kv)
-    return list(zip(out[:count], out[count:]))
-
-
-def attend_kernel(u, arrays, begun, table_ref, queries_ref, *refs):
+    )(table, *queries, kv, *held)
+    return list(zip(out[:count], out[count : 2 * count])), out[2 * count :]
+
+
+def attend_kernel(u, arrays, begin, begun, table_ref, queries_ref, *refs):
     kv_refs, refs = refs[:arrays], refs[arrays:]
     if begun:
         m_in, acc_in, *refs = refs
@@ -208,10 +218,13 @@
             at += ref.shape[0]
     else:
         kv_ref = kv_refs[0]
-    q_ref, s_ref, top_ref, m_ref, acc_ref = refs
-    total = table_ref[u, STEPS]
-
-    split_queries(queries_ref, q_ref)
+    halves = table_ref[u, STEPS]
+    if begun:
+        q_ref = queries_ref
+        s_ref, top_ref, m_ref, acc_ref = refs
+    else:
+        q_ref, s_ref, top_ref, m_ref, acc_ref = refs
+        split_queries(queries_ref, q_ref)
     if begun:
         m_ref[...] = m_in[...]
         acc_ref[...] = acc_in[...]
@@ -220,53 +233,75 @@
         acc_ref[...] = jnp.zeros((ROWS, 2 * HD), jnp.float32)
     above = above_diagonal()
 
-    def score(step, half):
-        score_step(table_ref, u, kv_ref, q_ref, step, above, s_ref.at[half], top_ref.at[half])
-
-    def absorb(step, half):
-        absorb_step(table_ref, u, kv_ref, step, s_ref.at[half], top_ref.at[half], m_ref, acc_ref)
-
-    @pl.when(total > 0)
-    def _():
-        score(0, 0)
-
-        def two(pair, carry):
-            step = 2 * pair
-            score(step + 1, 1)
-            absorb(step, 0)
-            score(step + 2, 0)
-            absorb(step + 1, 1)
-            return carry
-
-        lax.fori_loop(0, (total - 1) >> 1, two, 0)
-
-        @pl.when(total % 2 == 1)
+    def score(step, half, size=GROUP):
+        score_step(table_ref, u, kv_ref, q_ref, step, above, s_ref.at[half], top_ref.at[half], begin, size)
+
+    def absorb(step, half, size=GROUP):
+        absorb_step(table_ref, u, kv_ref, step, s_ref.at[half], top_ref.at[half], m_ref, acc_ref, begin, size)
+
+    if begun:
+        @pl.when(halves == 1)
         def _():
-            absorb(total - 1, 0)
-
-        @pl.when(total % 2 == 0)
+            score(0, 0, 2)
+            absorb(0, 0, 2)
+
+        @pl.when(halves == 2)
         def _():
-            score(total - 1, 1)
-            absorb(total - 2, 0)
-            absorb(total - 1, 1)
+            score(0, 0)
+            absorb(0, 0)
+
+        for last, size in ((3, 2), (4, GROUP)):
+
+            @pl.when(halves == last)
+            def _(size=size):
+                score(0, 0)
+                score(1, 1, size)
+                absorb(0, 0)
+                absorb(1, 1, size)
+    else:
+        total = (halves + 1) >> 1
+
+        @pl.when(total > 0)
+        def _():
+            score(0, 0)
+
+            def two(pair, carry):
+                step = 2 * pair
+                score(step + 1, 1)
+                absorb(step, 0)
+                score(step + 2, 0)
+                absorb(step + 1, 1)
+                return carry
+
+            lax.fori_loop(0, (total - 1) >> 1, two, 0)
+
+            @pl.when(total % 2 == 1)
+            def _():
+                absorb(total - 1, 0)
+
+            @pl.when(total % 2 == 0)
+            def _():
+                score(total - 1, 1)
+                absorb(total - 2, 0)
+                absorb(total - 1, 1)
 
     low = lax.broadcasted_iota(jnp.int32, (ROWS, HD), 1) < HD // 2
     out_ref[:ROWS, :] = acc_ref[:, :HD]
     out_ref[ROWS:, :] = jnp.where(low, m_ref[...], acc_ref[:, HD:])
 
 
-def attend(u, table, queries, arrays, state=()):
-    count = len(SLOTS)
+def attend(u, table, queries, arrays, begin=0, state=()):
+    count = sum(array.shape[0] for array in arrays) // SPAN
     out = [jax.ShapeDtypeStruct((2 * ROWS, HD), jnp.float32)]
     if len(arrays) > 1:
         out.append(jax.ShapeDtypeStruct((count * SPAN, 2 * HD), jnp.bfloat16))
     return pl.pallas_call(
-        functools.partial(attend_kernel, u, len(arrays), len(state) > 0),
+        functools.partial(attend_kernel, u, len(arrays), begin, len(state) > 0),
         out_shape=out,
         in_specs=[whole(pltpu.SMEM)] + [whole()] * (1 + len(arrays) + len(state)),
         out_specs=[whole()] * len(out),
-        scratch_shapes=[
-            VMEM((ROWS, 2 * HD), jnp.bfloat16),
+        scratch_shapes=([] if state else [VMEM((ROWS, 2 * HD), jnp.bfloat16)])
+        + [
             VMEM((2, ROWS, BLOCK), jnp.float32),
             VMEM((2, ROWS, HD), jnp.float32),
             VMEM((ROWS, HD), jnp.float32),
@@ -322,32 +357,64 @@
     )(near, far)
 
 
-def merge_kernel(near_ref, far_ref, beside_ref, out_ref):
-    parts = beside_ref[:, HEADS * HD :].astype(jnp.float32)
-    logs = parts + pltpu.roll(parts, HD - HEADS, 1) + pltpu.roll(parts, HD - 2 * HEADS, 1)
+def meet_kernel(near_ref, far_ref, value_ref, log_ref):
     for head in range(HEADS):
         rows = slice(head * SPAN, (head + 1) * SPAN)
         also = slice(ROWS + head * SPAN, ROWS + (head + 1) * SPAN)
-        columns = slice(head * HD, (head + 1) * HD)
         near, near_total = spread(near_ref[also, :])
         far, far_total = spread(far_ref[also, :])
-        beside = jnp.broadcast_to(logs[:, head : head + 1], (SPAN, HD))
-        top = jnp.maximum(jnp.maximum(near, far), beside)
-        near, far, beside = jnp.exp2(near - top), jnp.exp2(far - top), jnp.exp2(beside - top)
-        value = near_ref[rows, :] * near + far_ref[rows, :] * far + beside_ref[:, columns].astype(jnp.float32) * beside
-        out_ref[:, columns] = value / (near_total * near + far_total * far + beside)
-
-
-def merged(near, far, beside):
+        top = jnp.maximum(near, far)
+        near, far = jnp.exp2(near - top), jnp.exp2(far - top)
+        value = near_ref[rows, :] * near + far_ref[rows, :] * far
+        weight = near_total * near + far_total * far
+        live = weight > 0
+        safe = jnp.where(live, weight, 1.0)
+        value_ref[rows, :] = jnp.where(live, value / safe, 0.0)
+        log_ref[rows, :] = jnp.where(live, top + jnp.log(safe) * math.log2(math.e), NEVER)
+
+
+def met(near, far):
+    return pl.pallas_call(
+        meet_kernel,
+        out_shape=[jax.ShapeDtypeStruct((ROWS, HD), jnp.float32)] * 2,
+        in_specs=[whole()] * 2,
+        out_specs=[whole()] * 2,
+        compiler_params=limit(8),
+        name="meet",
+        cost_estimate=cost(8 * ROWS * HD, 24 * ROWS * HD, 2 * ROWS * HD),
+    )(near, far)
+
+
+def merge_kernel(value_ref, log_ref, beside_ref, out_ref, block_ref, done):
+    parts = beside_ref[:, HEADS * HD :].astype(jnp.float32)
+    logs = parts + pltpu.roll(parts, HD - HEADS, 1) + pltpu.roll(parts, HD - 2 * HEADS, 1)
+    copies = []
+    for head in range(HEADS):
+        rows = slice(head * SPAN, (head + 1) * SPAN)
+        columns = slice(head * HD, (head + 1) * HD)
+        near = log_ref[rows, :]
+        far = jnp.broadcast_to(logs[:, head : head + 1], (SPAN, HD))
+        top = jnp.maximum(near, far)
+        near, far = jnp.exp2(near - top), jnp.exp2(far - top)
+        value = value_ref[rows, :] * near + beside_ref[:, columns].astype(jnp.float32) * far
+        block_ref[head] = value / (near + far)
+        copies.append(pltpu.make_async_copy(block_ref.at[head], out_ref.at[:, columns], done.at[head]))
+        copies[-1].start()
+    for copy in copies:
+        copy.wait()
+
+
+def merged(value, log, beside):
     return pl.pallas_call(
         merge_kernel,
         out_shape=jax.ShapeDtypeStruct((SPAN, HEADS * HD), jnp.float32),
         in_specs=[whole()] * 3,
-        out_specs=whole(),
+        out_specs=whole(pltpu.HBM),
+        scratch_shapes=[VMEM((HEADS, SPAN, HD), jnp.float32), pltpu.SemaphoreType.DMA((HEADS,))],
         compiler_params=limit(8),
         name="merge",
-        cost_estimate=cost(8 * ROWS * HD, 20 * ROWS * HD, 2 * ROWS * HD),
-    )(near, far, beside)
+        cost_estimate=cost(8 * ROWS * HD, 16 * ROWS * HD, 2 * ROWS * HD),
+    )(value, log, beside)
 
 
 def together(keys, values):
@@ -362,22 +429,23 @@
     for d in (2, -1, 1):
         by_a[d] = send(kv, along_a(-d))
     table = lists(span_order)
+    partner = send(queries, ACROSS_CORE)
     beside_partner = send(beside, ACROSS_CORE)
     plane = jnp.concatenate([kv, *(by_a[d] for d in NEAR_A[1:])], axis=0)
     for d in (2, -1, 1):
         by_b[d] = send(plane, along_b(-d))
-    first, second = attend_near((5, 4), table, (beside_partner, beside), plane)
-    partner = send(queries, ACROSS_CORE)
-
-    arrays = [plane, *(by_b[d] for d in FAR_B)]
-    far, held = attend(BESIDE_PARTNER, table, beside_partner, arrays, first)
+    states, split = attend_early((5, 4), 0, table, (beside_partner, beside), plane)
+    (first, second), _ = attend_early((7, 6), 3 * NEAR, table, split, by_b[2], states)
+    pair = [by_b[-1], by_b[1]]
+    far, pair = attend(BESIDE_PARTNER, table, split[0], pair, NEAR, first)
     far = send(far, ACROSS_CORE)
-    (near,) = attend(BESIDE, table, beside, [held], second)
+    (near,) = attend(BESIDE, table, split[1], [pair], NEAR, second)
     back = send(joined(near, far), ACROSS_Y)
-    (far,) = attend(PARTNER, table, partner, [held])
+    far, held = attend(PARTNER, table, partner, [plane, pair, by_b[2]])
     far = send(far, ACROSS_CORE)
     (near,) = attend(OWN, table, queries, [held])
-    return merged(near, far, back)
+    value, log = met(near, far)
+    return merged(value, log, back)
 
 
 def solution(mesh):

time: 46.2 us -> 45 us (0.974); the launches traced: 45.3 us -> 44.8 us
  waiting for transfers between devices: 12.4 us -> 8.19 us
  starting transfers between devices: 14.9 us -> 17.1 us
  Pallas kernels: 17 us -> 18.4 us
    ppermute x12, waiting for transfers between devices: 12.4 us -> 8.19 us  [send(): return lax.ppermute(x, AXES, perm)]
    ppermute x12, starting transfers between devices: 14.9 us -> 17.1 us  [send(): return lax.ppermute(x, AXES, perm)]
    pallas_call x5 -> x7, Pallas kernels: 13.3 us -> 14.9 us  [the longest x4 9.46 us: attend(): pl.pallas_call(functools.partial(attend_kernel, u, len(arrays), begin, le...]
  transfers between devices with their start and end apart: 12 -> 12, of which waited for: 5 -> 3; matrix products, arithmetic and copies ran while one was open for 2% -> 2% of each run, Pallas kernels for 34% -> 39%
where the time goes in v1:
time: 45 us; the launch traced here: 44.8 us
  Pallas kernels  18.4 us (41%)
  starting transfers between devices  17.1 us (38%)
  waiting for transfers between devices  8.19 us (18%)
  other arithmetic  0.81 us (2%)
    ppermute x12, starting transfers between devices, send(): return lax.ppermute(x, AXES, perm)  17.1 us
    pallas_call x4, Pallas kernels, attend(): pl.pallas_call(functools.partial(attend_kernel, u, len(arrays), begin, le...  9.46 us
    ppermute x12, waiting for transfers between devices, send(): return lax.ppermute(x, AXES, perm)  8.19 us
    pallas_call x2, Pallas kernels, attend_early(): pl.pallas_call(functools.partial(early_kernel, lists_of, begin, len(held)...  4.97 us
    pallas_call x1, Pallas kernels, lists(): pl.pallas_call(lists_kernel, out_shape=jax.ShapeDtypeStruct((len(LISTS),...  1.68 us
    pallas_call x1, Pallas kernels, merged(): pl.pallas_call(merge_kernel, out_shape=jax.ShapeDtypeStruct((SPAN, HEADS...  1.07 us
  transfers between devices with their start and end apart: 12, of which 3 were waited for; matrix products, arithmetic and copies ran while one was open for 2% of the time, Pallas kernels for 39%

profile of v1, /device:TPU:0, one launch (start us, length us, event | category | flops | bytes accessed | tf_op | source)
XLA Modules:
  0.0 44.8 jit_solution(10683401428316793388)
XLA Ops:
  0.0 1.7 %collective-permute-start.4 = (bf16[128,1024]{1,0:T(8,128)(2,1)}, bf16[128,1024]{1,0:T(8,128)(2,1)S(1)}, u32[]{:S(2)}, u32[]{:S(2)}) collective-permute-start(bf16[128,1024]{1,0:T(8,128)(2,1)} %queries_ref.1), channel_id=1, source_target_pairs={{0,8},{1,9},{2,10},{3,11},{4,12},{5,13},{6,14},{7,15},{8,0},{9,1},... | collective-permute-start | bytes 786440 | tf_op jit(solution)/shard_map/ppermute | solution.py:50
  1.7 0.8 %pad_select_fusion = bf16[128,256]{1,0:T(8,128)(2,1)S(1)} fusion(bf16[128,128]{1,0:T(8,128)(2,1)} %param.6, bf16[128,128]{1,0:T(8,128)(2,1)} %param.5, pred[256]{0:T(512)(128)(4,1)S(1)} %iota_compare_fusion), kind=kLoop, calls=%fused_computation.1 | loop fusion | flops 32768 | bytes 131328 | tf_op jit(solution)/shard_map/jit(_where)/select_n | solution.py:422
  2.5 0.0 copy-start.1
  2.5 0.0 copy-start
  2.5 2.0 %collective-permute-start.1 = (bf16[128,256]{1,0:T(8,128)(2,1)S(1)}, bf16[128,256]{1,0:T(8,128)(2,1)S(1)}, u32[]{:S(2)}, u32[]{:S(2)}) collective-permute-start(bf16[128,256]{1,0:T(8,128)(2,1)S(1)} %pad_select_fusion), channel_id=1, source_target_pairs={{0,16},{1,3},{2,18},{3,5},{4,20},{5,7},{6,22},{7,1},{8,24},{9,11},... | collective-permute-start | bytes 196616 | tf_op jit(solution)/shard_map/ppermute | solution.py:50
  4.5 2.2 %collective-permute-start.2 = (bf16[128,256]{1,0:T(8,128)(2,1)S(1)}, bf16[128,256]{1,0:T(8,128)(2,1)S(1)}, u32[]{:S(2)}, u32[]{:S(2)}) collective-permute-start(bf16[128,256]{1,0:T(8,128)(2,1)S(1)} %pad_select_fusion), channel_id=1, source_target_pairs={{0,48},{1,7},{2,50},{3,1},{4,52},{5,3},{6,54},{7,5},{8,56},{9,15},... | collective-permute-start | bytes 196616 | tf_op jit(solution)/shard_map/ppermute | solution.py:50
  6.7 1.8 %collective-permute-start.3 = (bf16[128,256]{1,0:T(8,128)(2,1)S(1)}, bf16[128,256]{1,0:T(8,128)(2,1)S(1)}, u32[]{:S(2)}, u32[]{:S(2)}) collective-permute-start(bf16[128,256]{1,0:T(8,128)(2,1)S(1)} %pad_select_fusion), channel_id=1, source_target_pairs={{0,32},{1,5},{2,34},{3,7},{4,36},{5,1},{6,38},{7,3},{8,40},{9,13},... | collective-permute-start | bytes 196616 | tf_op jit(solution)/shard_map/ppermute | solution.py:50
  8.5 0.0 collective-permute-done.4.refs_1_
  8.5 0.0 collective-permute-start.5
  8.5 0.4 collective-permute-done.1
  8.9 0.0 collective-permute-done.2
  8.9 3.6 %collective-permute-done.3 = bf16[128,256]{1,0:T(8,128)(2,1)S(1)} collective-permute-done((bf16[128,256]{1,0:T(8,128)(2,1)S(1)}, bf16[128,256]{1,0:T(8,128)(2,1)S(1)}, u32[]{:S(2)}, u32[]{:S(2)}) %collective-permute-start.3) | collective-permute-done | bytes 65568 | tf_op jit(solution)/shard_map/ppermute | solution.py:50
  12.5 3.1 %collective-permute-start.8 = (bf16[512,256]{1,0:T(8,128)(2,1)S(1)}, bf16[512,256]{1,0:T(8,128)(2,1)S(1)}, u32[]{:S(2)}, u32[]{:S(2)}) collective-permute-start(bf16[512,256]{1,0:T(8,128)(2,1)S(1)} %pad_maximum_fusion.refs_2_.refs_0_), channel_id=1, source_target_pairs={{0,4},{1,33},{2,6},{3,35},{4,0},{5,37},{6,2},{7,39},{8,12},{9,41},... | collective-permute-start | bytes 786440 | tf_op jit(solution)/shard_map/ppermute | solution.py:50
  15.6 0.6 %collective-permute-start.6 = (bf16[512,256]{1,0:T(8,128)(2,1)S(1)}, bf16[512,256]{1,0:T(8,128)(2,1)S(1)}, u32[]{:S(2)}, u32[]{:S(2)}) collective-permute-start(bf16[512,256]{1,0:T(8,128)(2,1)S(1)} %pad_maximum_fusion.refs_2_.refs_0_), channel_id=1, source_target_pairs={{0,2},{1,17},{2,4},{3,19},{4,6},{5,21},{6,0},{7,23},{8,10},{9,25},... | collective-permute-start | bytes 786440 | tf_op jit(solution)/shard_map/ppermute | solution.py:50
  16.2 2.6 %collective-permute-start.7 = (bf16[512,256]{1,0:T(8,128)(2,1)S(1)}, bf16[512,256]{1,0:T(8,128)(2,1)S(1)}, u32[]{:S(2)}, u32[]{:S(2)}) collective-permute-start(bf16[512,256]{1,0:T(8,128)(2,1)S(1)} %pad_maximum_fusion.refs_2_.refs_0_), channel_id=1, source_target_pairs={{0,6},{1,49},{2,0},{3,51},{4,2},{5,53},{6,4},{7,55},{8,14},{9,57},... | collective-permute-start | bytes 786440 | tf_op jit(solution)/shard_map/ppermute | solution.py:50
  18.8 0.0 copy-done.1
  18.8 0.0 collective-permute-start
  18.8 0.0 copy-done
  18.8 1.7 %lists.1.table_ref = s32[8,64]{1,0:T(8,128)S(1)} custom-call(s32[64]{0:T(128)S(1)} %copy-done), custom_call_target="tpu_custom_call" | custom-call | flops 1024 | bytes 1024 | tf_op jit(solution)/shard_map/lists/pallas_call | solution.py:109
  20.5 0.0 collective-permute-done.5.refs_0_
  20.5 2.4 %shard_map.46 = (f32[1024,128]{1,0:T(8,128)S(1)}, f32[1024,128]{1,0:T(8,128)S(1)}, f32[1024,256]{1,0:T(8,128)S(1)}, f32[1024,256]{1,0:T(8,128)S(1)}, bf16[1024,2...) custom-call(s32[8,64]{1,0:T(8,128)S(1)} %lists.1.table_ref, bf16[128,1024]{1,0:T(8,128)(2,1)S(1)} %collective-permute-done.5.refs_0_, ...), custom_call_target="tpu_custom_call" | custom-call | flops 536870912 | bytes 524288 | tf_op jit(solution)/shard_map/pallas_call | solution.py:196
  23.0 0.0 collective-permute-done.8.refs_2_
  23.0 2.5 %shard_map.47 = (f32[1024,128]{1,0:T(8,128)S(1)}, f32[1024,128]{1,0:T(8,128)S(1)}, f32[1024,256]{1,0:T(8,128)S(1)}, f32[1024,256]{1,0:T(8,128)S(1)}) custom-call(s32[8,64]{1,0:T(8,128)S(1)} %lists.1.table_ref, bf16[1024,256]{1,0:T(8,128)(2,1)S(1)} %get-tuple-element.21.refs_0_.queries_ref, bf16[1024,256]{1,0:T(8,128)(2,1)S(1)} %get-tuple-element.22.refs_1_.queries_ref, ...), custom_call_target="tpu_custom_call" | custom-call | flops 536870912 | bytes 524288 | tf_op jit(solution)/shard_map/pallas_call | solution.py:196
  25.5 0.0 collective-permute-done.6.refs_0_
  25.5 0.0 collective-permute-done.7.refs_1_
  25.6 2.1 %shard_map.48 = (f32[2048,128]{1,0:T(8,128)S(1)}, bf16[1024,256]{1,0:T(8,128)(2,1)S(1)}) custom-call(s32[8,64]{1,0:T(8,128)S(1)} %lists.1.table_ref, bf16[1024,256]{1,0:T(8,128)(2,1)S(1)} %get-tuple-element.21.refs_0_.queries_ref, bf16[512,256]{1,0:T(8,128)(2,1)S(1)} %collective-permute-done.6.refs_0_, bf16[512,256]{1,0:T(8,128)(2,1)S(1)} %collective-permute-done.7.refs_1_, ...), custom_call_target="tpu_custom_call" | custom-call | flops 536870912 | bytes 524288 | tf_op jit(solution)/shard_map/pallas_call | solution.py:298
  27.6 0.3 collective-permute-start.10
  27.9 0.0 collective-permute-done.queries_ref
  27.9 2.0 %shard_map.49 = (f32[2048,128]{1,0:T(8,128)S(1)}, bf16[2048,256]{1,0:T(8,128)(2,1)S(1)}) custom-call(s32[8,64]{1,0:T(8,128)S(1)} %lists.1.table_ref, bf16[128,1024]{1,0:T(8,128)(2,1)S(1)} %collective-permute-done.queries_ref, bf16[512,256]{1,0:T(8,128)(2,1)S(1)} %pad_maximum_fusion.refs_2_.refs_0_, bf16[1024,256]{1,0:T(8,128)(2,1)S(1)} %get-tuple-element.29.refs_1_.refs_0_, ...), custom_call_target="tpu_custom_call" | custom-call | flops 1073741824 | bytes 1048576 | tf_op jit(solution)/shard_map/pallas_call | solution.py:298
  29.9 2.0 %collective-permute-start.9 = (f32[2048,128]{1,0:T(8,128)S(1)}, f32[2048,128]{1,0:T(8,128)S(1)}, u32[]{:S(2)}, u32[]{:S(2)}) collective-permute-start(f32[2048,128]{1,0:T(8,128)S(1)} %get-tuple-element.31), channel_id=1, source_target_pairs={{0,1},{1,0},{2,3},{3,2},{4,5},{5,4},{6,7},{7,6},{8,9},{9,8},{10,11... | collective-permute-start | bytes 3145736 | tf_op jit(solution)/shard_map/ppermute | solution.py:50
  31.9 2.0 %shard_map.51.near_ref = f32[2048,128]{1,0:T(8,128)S(1)} custom-call(s32[8,64]{1,0:T(8,128)S(1)} %lists.1.table_ref, bf16[1024,256]{1,0:T(8,128)(2,1)S(1)} %get-tuple-element.22.refs_1_.queries_ref, bf16[1024,256]{1,0:T(8,128)(2,1)S(1)} %get-tuple-element.29.refs_1_.refs_0_, f32[1024,128]{1,0:T(8,128)S(1)} %get-tuple-element.34.refs_1_, ...), custom_call_target="tpu_custom_call" | custom-call | flops 536870912 | bytes 524288 | tf_op jit(solution)/shard_map/pallas_call | solution.py:298
  33.9 0.0 collective-permute-done.10.far_ref
  33.9 0.7 %join.1 = bf16[128,1152]{1,0:T(8,128)(2,1)S(1)} custom-call(f32[2048,128]{1,0:T(8,128)S(1)} %shard_map.51.near_ref, f32[2048,128]{1,0:T(8,128)S(1)} %collective-permute-done.10.far_ref), custom_call_target="tpu_custom_call" | custom-call | flops 1048576 | bytes 2621440 | tf_op jit(solution)/shard_map/join/pallas_call | solution.py:349
  34.6 0.8 %collective-permute-start.11 = (bf16[128,1152]{1,0:T(8,128)(2,1)S(1)}, bf16[128,1152]{1,0:T(8,128)(2,1)S(1)}, u32[]{:S(2)}, u32[]{:S(2)}) collective-permute-start(bf16[128,1152]{1,0:T(8,128)(2,1)S(1)} %join.1), channel_id=1, source_target_pairs={{0,8},{1,9},{2,10},{3,11},{4,12},{5,13},{6,14},{7,15},{8,0},{9,1},... | collective-permute-start | bytes 884744 | tf_op jit(solution)/shard_map/ppermute | solution.py:50
  35.5 3.4 %shard_map.50.near_ref = f32[2048,128]{1,0:T(8,128)S(1)} custom-call(s32[8,64]{1,0:T(8,128)S(1)} %lists.1.table_ref, bf16[128,1024]{1,0:T(8,128)(2,1)S(1)} %copy-done.1, bf16[2048,256]{1,0:T(8,128)(2,1)S(1)} %get-tuple-element.30.refs_0_), custom_call_target="tpu_custom_call" | custom-call | flops 1073741824 | bytes 1048576 | tf_op jit(solution)/shard_map/pallas_call | solution.py:298
  38.8 0.0 collective-permute-done.9.far_ref
  38.9 0.5 %meet.1 = (f32[1024,128]{1,0:T(8,128)S(1)}, f32[1024,128]{1,0:T(8,128)S(1)}) custom-call(f32[2048,128]{1,0:T(8,128)S(1)} %shard_map.50.near_ref, f32[2048,128]{1,0:T(8,128)S(1)} %collective-permute-done.9.far_ref), custom_call_target="tpu_custom_call" | custom-call | flops 1048576 | bytes 3145728 | tf_op jit(solution)/shard_map/meet/pallas_call | solution.py:377
  39.4 4.2 %collective-permute-done.11.beside_ref = bf16[128,1152]{1,0:T(8,128)(2,1)S(1)} collective-permute-done((bf16[128,1152]{1,0:T(8,128)(2,1)S(1)}, bf16[128,1152]{1,0:T(8,128)(2,1)S(1)}, u32[]{:S(2)}, u32[]{:S(2)}) %collective-permute-start.11) | collective-permute-done | bytes 294944 | tf_op jit(solution)/shard_map/ppermute | solution.py:50
  43.6 1.1 %merge.1 = f32[128,1024]{1,0:T(8,128)} custom-call(f32[1024,128]{1,0:T(8,128)S(1)} %get-tuple-element.32.value_ref, f32[1024,128]{1,0:T(8,128)S(1)} %get-tuple-element.33.log_ref, bf16[128,1152]{1,0:T(8,128)(2,1)S(1)} %collective-permute-done.11.beside_ref), custom_call_target="tpu_custom_call" | custom-call | flops 1048576 | bytes 2097152 | tf_op jit(solution)/shard_map/merge/pallas_call | solution.py:408
  (2 shorter events, 0.0 us)
Async XLA Ops:
  0.0 8.5 %collective-permute-start.4 = (bf16[128,1024]{1,0:T(8,128)(2,1)}, bf16[128,1024]{1,0:T(8,128)(2,1)S(1)}, u32[]{:S(2)}, u32[]{:S(2)}) collective-permute-start(bf16[128,1024]{1,0:T(8,128)(2,1)} %queries_ref.1), channel_id=1, source_target_pairs={{0,8},{1,9},{2,10},{3,11},{4,12},{5,13},{6,14},{7,15},{8,0},{9,1},... | collective-permute-start | bytes 786440 | tf_op jit(solution)/shard_map/ppermute | solution.py:50
  2.5 16.3 %copy-start.1 = (bf16[128,1024]{1,0:T(8,128)(2,1)S(1)}, bf16[128,1024]{1,0:T(8,128)(2,1)}, u32[]{:S(2)}) copy-start(bf16[128,1024]{1,0:T(8,128)(2,1)} %queries_ref.1) | copy-start | bytes 786436
  2.5 16.3 %copy-start = (s32[64]{0:T(128)S(1)}, s32[64]{0:T(128)}, u32[]{:S(2)}) copy-start(s32[64]{0:T(128)} %order_ref.1) | copy-start | bytes 772
  2.5 6.4 %collective-permute-start.1 = (bf16[128,256]{1,0:T(8,128)(2,1)S(1)}, bf16[128,256]{1,0:T(8,128)(2,1)S(1)}, u32[]{:S(2)}, u32[]{:S(2)}) collective-permute-start(bf16[128,256]{1,0:T(8,128)(2,1)S(1)} %pad_select_fusion), channel_id=1, source_target_pairs={{0,16},{1,3},{2,18},{3,5},{4,20},{5,7},{6,22},{7,1},{8,24},{9,11},... | collective-permute-start | bytes 196616 | tf_op jit(solution)/shard_map/ppermute | solution.py:50
  4.5 4.4 %collective-permute-start.2 = (bf16[128,256]{1,0:T(8,128)(2,1)S(1)}, bf16[128,256]{1,0:T(8,128)(2,1)S(1)}, u32[]{:S(2)}, u32[]{:S(2)}) collective-permute-start(bf16[128,256]{1,0:T(8,128)(2,1)S(1)} %pad_select_fusion), channel_id=1, source_target_pairs={{0,48},{1,7},{2,50},{3,1},{4,52},{5,3},{6,54},{7,5},{8,56},{9,15},... | collective-permute-start | bytes 196616 | tf_op jit(solution)/shard_map/ppermute | solution.py:50
  6.7 5.8 %collective-permute-start.3 = (bf16[128,256]{1,0:T(8,128)(2,1)S(1)}, bf16[128,256]{1,0:T(8,128)(2,1)S(1)}, u32[]{:S(2)}, u32[]{:S(2)}) collective-permute-start(bf16[128,256]{1,0:T(8,128)(2,1)S(1)} %pad_select_fusion), channel_id=1, source_target_pairs={{0,32},{1,5},{2,34},{3,7},{4,36},{5,1},{6,38},{7,3},{8,40},{9,13},... | collective-permute-start | bytes 196616 | tf_op jit(solution)/shard_map/ppermute | solution.py:50
  8.5 12.1 %collective-permute-start.5 = (bf16[128,1024]{1,0:T(8,128)(2,1)S(1)}, bf16[128,1024]{1,0:T(8,128)(2,1)S(1)}, u32[]{:S(2)}, u32[]{:S(2)}) collective-permute-start(bf16[128,1024]{1,0:T(8,128)(2,1)S(1)} %collective-permute-done.4.refs_1_), channel_id=1, source_target_pairs={{0,1},{1,0},{2,3},{3,2},{4,5},{5,4},{6,7},{7,6},{8,9},{9,8},{10,11... | collective-permute-start | bytes 786440 | tf_op jit(solution)/shard_map/ppermute | solution.py:50
  12.5 10.5 %collective-permute-start.8 = (bf16[512,256]{1,0:T(8,128)(2,1)S(1)}, bf16[512,256]{1,0:T(8,128)(2,1)S(1)}, u32[]{:S(2)}, u32[]{:S(2)}) collective-permute-start(bf16[512,256]{1,0:T(8,128)(2,1)S(1)} %pad_maximum_fusion.refs_2_.refs_0_), channel_id=1, source_target_pairs={{0,4},{1,33},{2,6},{3,35},{4,0},{5,37},{6,2},{7,39},{8,12},{9,41},... | collective-permute-start | bytes 786440 | tf_op jit(solution)/shard_map/ppermute | solution.py:50
  15.6 9.9 %collective-permute-start.6 = (bf16[512,256]{1,0:T(8,128)(2,1)S(1)}, bf16[512,256]{1,0:T(8,128)(2,1)S(1)}, u32[]{:S(2)}, u32[]{:S(2)}) collective-permute-start(bf16[512,256]{1,0:T(8,128)(2,1)S(1)} %pad_maximum_fusion.refs_2_.refs_0_), channel_id=1, source_target_pairs={{0,2},{1,17},{2,4},{3,19},{4,6},{5,21},{6,0},{7,23},{8,10},{9,25},... | collective-permute-start | bytes 786440 | tf_op jit(solution)/shard_map/ppermute | solution.py:50
  16.2 9.4 %collective-permute-start.7 = (bf16[512,256]{1,0:T(8,128)(2,1)S(1)}, bf16[512,256]{1,0:T(8,128)(2,1)S(1)}, u32[]{:S(2)}, u32[]{:S(2)}) collective-permute-start(bf16[512,256]{1,0:T(8,128)(2,1)S(1)} %pad_maximum_fusion.refs_2_.refs_0_), channel_id=1, source_target_pairs={{0,6},{1,49},{2,0},{3,51},{4,2},{5,53},{6,4},{7,55},{8,14},{9,57},... | collective-permute-start | bytes 786440 | tf_op jit(solution)/shard_map/ppermute | solution.py:50
  18.8 9.1 %collective-permute-start = (bf16[128,1024]{1,0:T(8,128)(2,1)S(1)}, bf16[128,1024]{1,0:T(8,128)(2,1)S(1)}, u32[]{:S(2)}, u32[]{:S(2)}) collective-permute-start(bf16[128,1024]{1,0:T(8,128)(2,1)S(1)} %copy-done.1), channel_id=1, source_target_pairs={{0,1},{1,0},{2,3},{3,2},{4,5},{5,4},{6,7},{7,6},{8,9},{9,8},{10,11... | collective-permute-start | bytes 786440 | tf_op jit(solution)/shard_map/ppermute | solution.py:50
  27.6 6.3 %collective-permute-start.10 = (f32[2048,128]{1,0:T(8,128)S(1)}, f32[2048,128]{1,0:T(8,128)S(1)}, u32[]{:S(2)}, u32[]{:S(2)}) collective-permute-start(f32[2048,128]{1,0:T(8,128)S(1)} %get-tuple-element.36), channel_id=1, source_target_pairs={{0,1},{1,0},{2,3},{3,2},{4,5},{5,4},{6,7},{7,6},{8,9},{9,8},{10,11... | collective-permute-start | bytes 3145736 | tf_op jit(solution)/shard_map/ppermute | solution.py:50
  29.9 8.9 %collective-permute-start.9 = (f32[2048,128]{1,0:T(8,128)S(1)}, f32[2048,128]{1,0:T(8,128)S(1)}, u32[]{:S(2)}, u32[]{:S(2)}) collective-permute-start(f32[2048,128]{1,0:T(8,128)S(1)} %get-tuple-element.31), channel_id=1, source_target_pairs={{0,1},{1,0},{2,3},{3,2},{4,5},{5,4},{6,7},{7,6},{8,9},{9,8},{10,11... | collective-permute-start | bytes 3145736 | tf_op jit(solution)/shard_map/ppermute | solution.py:50
  34.6 8.9 %collective-permute-start.11 = (bf16[128,1152]{1,0:T(8,128)(2,1)S(1)}, bf16[128,1152]{1,0:T(8,128)(2,1)S(1)}, u32[]{:S(2)}, u32[]{:S(2)}) collective-permute-start(bf16[128,1152]{1,0:T(8,128)(2,1)S(1)} %join.1), channel_id=1, source_target_pairs={{0,8},{1,9},{2,10},{3,11},{4,12},{5,13},{6,14},{7,15},{8,0},{9,1},... | collective-permute-start | bytes 884744 | tf_op jit(solution)/shard_map/ppermute | solution.py:50
